TPU v7x, 32 devices: a whole 2x2x4 slice. The times are simulated.
32 devices in a mesh: dp: 8 (over z, y), tensor: 4 (over x, core).
Axes of the slice: x: 2, y: 2, z: 4, core: 2. Of those that a mesh axis runs over, the one named last changes fastest.
Arguments:
- tokens: bfloat16 [3152, 768], P('dp'), may hold values from -6 to 6
- norm_params: float32 [4, 768], replicated, may hold values from 0.5 to 1.5
- w_qkv: bfloat16 [3, 768, 768], P(None, None, 'tensor'), may hold values from -0.21875 to 0.21875
- b_qv: float32 [2, 768], P(None, 'tensor'), may hold values from -3 to 3
- w_out: bfloat16 [768, 768], P('tensor'), may hold values from -1.75 to 1.75
- b_out: float32 [768], replicated, may hold values from -3 to 3
- w_router: bfloat16 [768, 4], replicated, may hold values from -0.4375 to 0.4375
- w_in: bfloat16 [4, 768, 3072], P(None, None, 'tensor'), may hold values from -0.21875 to 0.21875
- b_in: float32 [4, 3072], P(None, 'tensor'), may hold values from -3 to 3
- w_back: bfloat16 [4, 3072, 768], P(None, 'tensor'), may hold values from -0.3125 to 0.3125
- b_back: float32 [4, 768], replicated, may hold values from -3 to 3
- routes: int32 [3152, 2], P('dp'), may hold values from 0 to 3, all different within a row; in each aligned block of 394 rows (0 to 393, 394 to 787, ...) at most 263 rows name the same one
- img_count: int32 [8], P('dp'), may hold values from 1 to 2, as said below
- cotangent: bfloat16 [3152, 768], P('dp'), may hold values from -6 to 6
Outputs:
- out_act: bfloat16 [3152, 768], P('dp')
- in_grad: float32 [3152, 768], P('dp')
- g_norms: float32 [4, 768], replicated
- g_qkv: float32 [3, 768, 768], P(None, 'dp', 'tensor')
- g_qv: float32 [2, 768], P(None, 'tensor')
- g_out: float32 [768, 768], P('tensor', 'dp')
- g_bout: float32 [768], replicated
- g_router: float32 [768, 4], replicated
- g_in: float32 [4, 768, 3072], P(None, 'dp', 'tensor')
- g_bin: float32 [4, 3072], P(None, 'tensor')
- g_back: float32 [4, 3072, 768], P(None, 'tensor', 'dp')
- g_bback: float32 [4, 768], replicated
Inputs may be any that keep to these rules, and one draw needn't show every extreme that they name: In the rows of one group of devices along dp no expert is named by more than 263 routes; the two experts of a token differ. The first img_count[g] image slots of group g hold live images, the rest are empty.
All inputs are finite; a program needn't handle non-finite values.
Results may differ from a plain program's by a relative error of at most 0.028.
The roundings to bfloat16 on the way count: a program that leaves them out, or rounds other values in their place, can miss the bound.
Values sent between devices are 32-bit elements; how exact they have to be, the bound alone decides.
No kernel may reach another device: no remote copies, remote signals or barrier semaphores. Data moves between devices by JAX's collectives and lax.ppermute only.
A program may use at most 128 MiB of HBM per device.

v0:
```python
import jax
import jax.numpy as jnp
from jax import lax
from jax.sharding import PartitionSpec as P

HD = 64
SEQ = 197
CAP = 263


EPS = 1e-06


def normalize(value, gain, shift):
    mean_v = jnp.mean(value, -1, keepdims=True)
    centred = value - mean_v
    inv_std = lax.rsqrt(jnp.mean(centred * centred, -1, keepdims=True) + EPS)
    normed = centred * inv_std
    return (normed * gain + shift, normed, inv_std)


def norm_back(grad, normed, inv_std, gain):
    scaled = grad * gain
    inner = jnp.mean(scaled * normed, -1, keepdims=True)
    return (scaled - jnp.mean(scaled, -1, keepdims=True) - normed * inner) * inv_std


def gelu_exact(value):
    return jax.nn.gelu(value, approximate=False)


def body(
    tokens,
    norm_params,
    w_qkv,
    b_qv,
    w_out,
    b_out,
    w_router,
    w_in,
    b_in,
    w_back,
    b_back,
    routes,
    img_count,
    cotangent,
):
    row_count, width = tokens.shape
    images = row_count // SEQ
    heads_loc = w_qkv.shape[2] // HD
    experts = w_in.shape[0]
    scale = HD ** (-0.5)
    x_full = tokens.astype(jnp.float32)
    slot_of = jnp.arange(row_count, dtype=jnp.int32) // SEQ
    live = (slot_of < img_count[0]).astype(jnp.float32)[:, None]
    grad_y = cotangent.astype(jnp.float32) * live
    norm_one, normed_one, inv_one = normalize(x_full, norm_params[0], norm_params[1])
    act_one = norm_one.astype(jnp.bfloat16)
    project = jnp.einsum("rd,jdc->jrc", act_one, w_qkv, preferred_element_type=jnp.float32)
    q_loc = (project[0] + b_qv[0]).astype(jnp.bfloat16).reshape(images, SEQ, heads_loc, HD)
    k_loc = project[1].astype(jnp.bfloat16).reshape(images, SEQ, heads_loc, HD)
    v_loc = (project[2] + b_qv[1]).astype(jnp.bfloat16).reshape(images, SEQ, heads_loc, HD)
    scores = scale * jnp.einsum("iqhd,ikhd->ihqk", q_loc, k_loc, preferred_element_type=jnp.float32)
    log_total = jax.nn.logsumexp(scores, axis=-1, keepdims=True)
    probs_low = jnp.exp(scores - log_total).astype(jnp.bfloat16)
    context = jnp.einsum("ihqk,ikhd->iqhd", probs_low, v_loc, preferred_element_type=jnp.float32)
    context = context.astype(jnp.bfloat16).reshape(row_count, heads_loc * HD)
    attn = lax.psum(jnp.dot(context, w_out, preferred_element_type=jnp.float32), "tensor")
    hidden = x_full + attn + b_out
    norm_two, normed_two, inv_two = normalize(hidden, norm_params[2], norm_params[3])
    act_two = norm_two.astype(jnp.bfloat16)
    logits = jnp.dot(act_two, w_router, preferred_element_type=jnp.float32)
    gates = jax.nn.softmax(logits, axis=-1)
    pick_int = (routes[:, :, None] == jnp.arange(experts, dtype=jnp.int32)[None, None, :]).astype(
        jnp.int32
    )
    picks = pick_int.astype(jnp.float32)
    gate_k = jnp.sum(picks * gates[:, None, :], -1)
    flat_pick = pick_int.reshape(row_count * 2, experts)
    position = jnp.sum((jnp.cumsum(flat_pick, 0) - flat_pick) * flat_pick, -1)
    slot_id = routes.reshape(-1) * CAP + position
    token_of = (
        jnp.full((experts * CAP,), row_count, jnp.int32)
        .at[slot_id]
        .set(jnp.arange(row_count * 2, dtype=jnp.int32) // 2)
    )
    padded = jnp.concatenate([act_two, jnp.zeros((1, width), jnp.bfloat16)], 0)
    dispatched = padded[token_of].reshape(experts, CAP, width)
    pre_act = (
        jnp.einsum("ecd,edf->ecf", dispatched, w_in, preferred_element_type=jnp.float32)
        + b_in[:, None, :]
    )
    hidden_low = gelu_exact(pre_act).astype(jnp.bfloat16)
    expert_out = jnp.einsum(
        "ecf,efd->ecd", hidden_low, w_back, preferred_element_type=jnp.float32
    ).reshape(experts * CAP, width)
    route_out = expert_out[slot_id].reshape(row_count, 2, width)
    moe_part = jnp.sum(gate_k[:, :, None] * route_out, 1)
    dots_part = jnp.sum(route_out * grad_y[:, None, :], -1)
    moe, dots = lax.psum((moe_part, dots_part), "tensor")
    bias_route = jnp.einsum("rke,ed->rkd", picks, b_back)
    moe_total = moe + jnp.sum(gate_k[:, :, None] * bias_route, 1)
    out_act = ((hidden + moe_total) * live).astype(jnp.bfloat16)
    dgate = dots + jnp.sum(bias_route * grad_y[:, None, :], -1)
    g_bback = jnp.einsum("rke,rd->ed", picks * gate_k[:, :, None], grad_y)
    du_route = (
        (gate_k[:, :, None] * grad_y[:, None, :]).astype(jnp.bfloat16).reshape(row_count * 2, width)
    )
    du_slots = (
        jnp.zeros((experts * CAP, width), jnp.bfloat16)
        .at[slot_id]
        .set(du_route)
        .reshape(experts, CAP, width)
    )
    g_back = jnp.einsum("ecf,ecd->efd", hidden_low, du_slots, preferred_element_type=jnp.float32)
    dhidden = jnp.einsum("ecd,efd->ecf", du_slots, w_back, preferred_element_type=jnp.float32)
    _, gelu_pull = jax.vjp(gelu_exact, pre_act)
    dpre = gelu_pull(dhidden)[0].astype(jnp.bfloat16)
    g_bin = jnp.sum(dpre.astype(jnp.float32), 1)
    g_in = jnp.einsum("ecd,ecf->edf", dispatched, dpre, preferred_element_type=jnp.float32)
    dslots = jnp.einsum("ecf,edf->ecd", dpre, w_in, preferred_element_type=jnp.float32).reshape(
        experts * CAP, width
    )
    da2_part = jnp.sum(dslots[slot_id].reshape(row_count, 2, width), 1)
    dgates = jnp.einsum("rk,rke->re", dgate, picks)
    dlogits = gates * (dgates - jnp.sum(gates * dgates, -1, keepdims=True))
    dlog_low = dlogits.astype(jnp.bfloat16)
    g_router = jnp.einsum("rd,re->de", act_two, dlog_low, preferred_element_type=jnp.float32)
    router_back = jnp.einsum("re,de->rd", dlog_low, w_router, preferred_element_type=jnp.float32)
    da_two = lax.psum(da2_part, "tensor") + router_back
    g_gain_two = jnp.sum(da_two * normed_two, 0)
    g_shift_two = jnp.sum(da_two, 0)
    dhid = grad_y + norm_back(da_two, normed_two, inv_two, norm_params[2])
    g_bout = jnp.sum(dhid, 0)
    dhid_low = dhid.astype(jnp.bfloat16)
    g_out = jnp.einsum("rc,rd->cd", context, dhid_low, preferred_element_type=jnp.float32)
    dcontext = jnp.einsum("rd,cd->rc", dhid_low, w_out, preferred_element_type=jnp.float32)
    dcontext = dcontext.astype(jnp.bfloat16).reshape(images, SEQ, heads_loc, HD)
    again = scale * jnp.einsum("iqhd,ikhd->ihqk", q_loc, k_loc, preferred_element_type=jnp.float32)
    probs = jnp.exp(again - log_total)
    dprobs = jnp.einsum("iqhd,ikhd->ihqk", dcontext, v_loc, preferred_element_type=jnp.float32)
    dv_loc = jnp.einsum(
        "ihqk,iqhd->ikhd", probs.astype(jnp.bfloat16), dcontext, preferred_element_type=jnp.float32
    ).astype(jnp.bfloat16)
    dscore = (probs * (dprobs - jnp.sum(probs * dprobs, -1, keepdims=True))).astype(jnp.bfloat16)
    dq_loc = (
        scale * jnp.einsum("ihqk,ikhd->iqhd", dscore, k_loc, preferred_element_type=jnp.float32)
    ).astype(jnp.bfloat16)
    dk_loc = (
        scale * jnp.einsum("ihqk,iqhd->ikhd", dscore, q_loc, preferred_element_type=jnp.float32)
    ).astype(jnp.bfloat16)
    dstack = jnp.stack([dq_loc, dk_loc, dv_loc], 0).reshape(3, row_count, heads_loc * HD)
    g_qkv = jnp.einsum("rd,jrc->jdc", act_one, dstack, preferred_element_type=jnp.float32)
    g_qv = jnp.stack(
        [jnp.sum(dstack[0].astype(jnp.float32), 0), jnp.sum(dstack[2].astype(jnp.float32), 0)], 0
    )
    da1_part = jnp.einsum("jrc,jdc->rd", dstack, w_qkv, preferred_element_type=jnp.float32)
    da_one = lax.psum(da1_part, "tensor")
    g_gain_one = jnp.sum(da_one * normed_one, 0)
    g_shift_one = jnp.sum(da_one, 0)
    in_grad = dhid + norm_back(da_one, normed_one, inv_one, norm_params[0])
    g_norms = jnp.stack([g_gain_one, g_shift_one, g_gain_two, g_shift_two], 0)
    g_qkv_s, g_out_s, g_in_s, g_back_s = (
        lax.psum_scatter(g_qkv, "dp", scatter_dimension=1, tiled=True),
        lax.psum_scatter(g_out, "dp", scatter_dimension=1, tiled=True),
        lax.psum_scatter(g_in, "dp", scatter_dimension=1, tiled=True),
        lax.psum_scatter(g_back, "dp", scatter_dimension=2, tiled=True),
    )
    g_norms_s, g_qv_s, g_bout_s, g_router_s, g_bin_s, g_bback_s = lax.psum(
        (g_norms, g_qv, g_bout, g_router, g_bin, g_bback), "dp"
    )
    return (
        out_act,
        in_grad,
        g_norms_s,
        g_qkv_s,
        g_qv_s,
        g_out_s,
        g_bout_s,
        g_router_s,
        g_in_s,
        g_bin_s,
        g_back_s,
        g_bback_s,
    )


def solution(mesh):
    placed = (
        P("dp", None),
        P(),
        P(None, None, "tensor"),
        P(None, "tensor"),
        P("tensor", None),
        P(),
        P(),
        P(None, None, "tensor"),
        P(None, "tensor"),
        P(None, "tensor", None),
        P(),
        P("dp", None),
        P("dp"),
        P("dp", None),
    )
    return jax.shard_map(
        body,
        mesh=mesh,
        in_specs=placed,
        out_specs=(
            P("dp", None),
            P("dp", None),
            P(),
            P(None, "dp", "tensor"),
            P(None, "tensor"),
            P("tensor", "dp"),
            P(),
            P(),
            P(None, "dp", "tensor"),
            P(None, "tensor"),
            P(None, "tensor", "dp"),
            P(),
        ),
        check_vma=False,
    )
```

profile of v0, /device:TPU:0, one launch (start us, length us, event | category | flops | bytes accessed | tf_op | source)
XLA Modules:
  0.0 708.4 jit_solution(7974491306480820455)
XLA Ops:
  24.4 4.2 mul.278
  28.7 5.5 scatter_custom_fusion
  35.4 24.3 %all-reduce.8.cloned.1.call-done = f32[394,768]{1,0:T(8,128)} async-done(((f32[394,768]{1,0:T(8,128)}), f32[394,768]{1,0:T(8,128)}) %all-reduce.8.cloned.1.call-update) | async-done | bytes 1210384 | tf_op jit(solution)/shard_map/psum | solution.py:68
  64.7 4.9 gather_fusion
  69.7 3.1 reshape.223
  72.7 11.2 %scatter_custom_fusion.1 = bf16[1052,768]{1,0:T(8,128)(2,1)} fusion(s32[788]{0:T(1024)} %copy-done.60, f32[788,768]{1,0:T(8,128)} %mul.278, f32[788]{0:T(1024)S(1)} %copy-done.56, bf16[]{:T(256)} %constant.50.clone.1), kind=kCustom, calls=%fused_computation.66 | custom fusion | flops 1210368 | bytes 4052560 | tf_op jit(solution)/shard_map/scatter | solution.py:112
  83.9 3.1 reshape.226
  87.0 5.2 fusion.32
  92.2 12.0 %convert_reduce_fusion = (f32[4,768]{1,0:T(4,128)}, bf16[4,263,768]{2,1,0:T(8,128)(2,1)S(1)}, f32[4,263,768]{2,1,0:T(8,128)S(1)}) fusion(f32[4,263,768]{2,1,0:T(8,128)S(1)} %get-tuple-element.93, f32[4,768]{1,0:T(4,128)S(1)} %copy-done.62, u8[263,768]{1,0:T(8,128)(4,1)S(1)} %get-tuple-element.49, u8[263,768]{1,0:T(8,128)(4,1)S(1)} %get-tuple-element.48, ...), kind=kOutput, calls=%fused_computation.12 | convolution fusion | flops 1305621504 | bytes 14842368 | tf_op jit(solution)/shard_map/ecd,efd->ecf/dot_general | solution.py:116
  105.9 3.2 fusion.85
  109.1 4.0 reshape.227
  113.1 6.7 gather_fusion.2
  119.8 4.0 reshape.228
  123.8 5.7 reduce_sum.265
  129.7 6.0 fusion.84
  135.7 4.0 reshape.224
  139.7 6.7 gather_fusion.1
  146.4 4.2 reshape.225
  150.5 4.6 multiply_reduce_fusion.1
  155.1 6.5 psum.80
  164.3 3.6 all-reduce.10.cloned.1.call-done
  188.0 4.2 copy.88
  192.2 4.6 reshape.279
  196.9 8.2 %fusion.87 = f32[4,768,768]{2,1,0:T(8,128)} fusion(bf16[4,263,768]{2,1,0:T(8,128)(2,1)} %reshape.223, bf16[4,263,768]{2,1,0:T(8,128)(2,1)} %copy-done.9), kind=kOutput, calls=%fused_computation.181 | convolution fusion | flops 1240989696 | bytes 12668928 | tf_op jit(solution)/shard_map/ecd,ecf->edf/dot_general | solution.py:120
  205.2 8.3 %fusion.88 = f32[4,768,768]{1,2,0:T(8,128)} fusion(bf16[4,263,768]{2,1,0:T(8,128)(2,1)} %multiply_convert_fusion, bf16[4,263,768]{2,1,0:T(8,128)(2,1)} %reshape.226), kind=kOutput, calls=%fused_computation.182 | convolution fusion | flops 1240989696 | bytes 12668928 | tf_op jit(solution)/shard_map/ecf,ecd->efd/dot_general | solution.py:115
  216.0 22.2 %reduce-scatter.15.cloned.1.call-done = f32[96,192]{1,0:T(8,128)} async-done(((f32[768,192]{1,0:T(8,128)}), f32[96,192]{1,0:T(8,128)}) %reduce-scatter.15.cloned.1.call-update) | async-done | bytes 73744
  239.9 57.7 %all-reduce.12.cloned.1.call-done = (f32[394,768]{1,0:T(8,128)}, f32[394,768]{1,0:T(8,128)}) async-done(((f32[394,768]{1,0:T(8,128)}, f32[394,768]{1,0:T(8,128)}), (f32[394,768]{1,0:T(8,128)}, f32[394,768]{1,0:T(8,128)})) %all-reduce.12.cloned.1.call-update) | async-done | bytes 2420752 | tf_op jit(solution)/shard_map/psum | solution.py:100
  299.6 38.6 %all-reduce.2 = (f32[4,768]{1,0:T(4,128)}, f32[2,192]{1,0:T(2,128)}, f32[768]{0:T(1024)}, f32[768,4]{0,1:T(4,128)}, f32[4,768]{1,0:T(4,128)}, /*index=5*/f32[4,768]{1,0:T(4,128)}) all-reduce(f32[4,768]{1,0:T(4,128)S(1)} %pad_maximum_fusion, f32[2,192]{1,0:T(2,128)S(1)} %pad_maximum_fusion.1, ...), channel_id=1, replica_groups=mesh['dp'=8,'tensor'=4] {'dp'}, use_global_device_ids=true, to_apply=%region_34.35 | all-reduce | flops 13440 | bytes 107520 | tf_op jit(solution)/shard_map/psum | solution.py:169
  338.2 2.9 multiply_convert_fusion.3
  342.6 25.6 %reduce-scatter.13.cloned.1.call-done = f32[96,576]{1,0:T(8,128)} async-done(((f32[768,576]{1,0:T(8,128)}), f32[96,576]{1,0:T(8,128)}) %reduce-scatter.13.cloned.1.call-update) | async-done | bytes 221200
  370.0 164.6 %reduce-scatter.9.cloned.1.call-done = f32[4,96,768]{2,1,0:T(8,128)} async-done(((f32[4,768,768]{2,1,0:T(8,128)}), f32[4,96,768]{2,1,0:T(8,128)}) %reduce-scatter.9.cloned.1.call-update) | async-done | bytes 1179664 | tf_op jit(solution)/shard_map/reduce_scatter | solution.py:166
  534.6 166.7 %reduce-scatter.11.cloned.1.call-done = f32[4,768,96]{1,2,0:T(8,128)} async-done(((f32[4,768,768]{1,2,0:T(8,128)}), f32[4,768,96]{1,2,0:T(8,128)}) %reduce-scatter.11.cloned.1.call-update) | async-done | bytes 1179664 | tf_op jit(solution)/shard_map/reduce_scatter | solution.py:167
  (256 shorter events, 56.3 us)
Async XLA Ops:
  7.2 4.3 copy-start
  7.2 52.5 %all-reduce.8.cloned.1.call-start = ((), (), s32[]{:S(2)}) async-start(), calls=%async_computation.4 | async-start | bytes 2457600 | tf_op jit(solution)/shard_map/psum | solution.py:68
  8.6 4.8 copy-start.44
  10.0 3.4 copy-start.49
  11.5 50.1 %copy-start.31 = (f32[768]{0:T(1024)}, f32[768]{0:T(1024)S(1)}, u32[]{:S(2)}) copy-start(f32[768]{0:T(1024)S(1)} %get-tuple-element.64) | copy-start | bytes 9220
  17.4 4.2 copy-start.14
  18.9 149.1 %all-reduce.10.cloned.1.call-start = ((), (), s32[]{:S(2)}) async-start(), calls=%async_computation.5 | async-start | bytes 2457600 | tf_op jit(solution)/shard_map/psum | solution.py:130
  19.8 4.7 copy-start.38
  24.4 35.3 %copy-start.5 = (bf16[394,768]{1,0:T(8,128)(2,1)S(1)}, bf16[394,768]{1,0:T(8,128)(2,1)}, u32[]{:S(2)}) copy-start(bf16[394,768]{1,0:T(8,128)(2,1)} %param.14) | copy-start | bytes 1815556
  24.4 35.3 %copy-start.65 = (f32[768]{0:T(1024)S(1)}, f32[768]{0:T(1024)}, u32[]{:S(2)}) copy-start(f32[768]{0:T(1024)} %param.19) | copy-start | bytes 9220
  28.7 32.6 %copy-start.60 = (s32[788]{0:T(1024)}, s32[788]{0:T(1024)S(1)}, u32[]{:S(2)}) copy-start(s32[788]{0:T(1024)S(1)} %fusion.63) | copy-start | bytes 9460
  62.5 7.2 %copy-start.10 = (bf16[394,768]{1,0:T(8,128)(2,1)}, bf16[394,768]{1,0:T(8,128)(2,1)S(1)}, u32[]{:S(2)}) copy-start(bf16[394,768]{1,0:T(8,128)(2,1)S(1)} %add_convert_fusion.1) | copy-start | bytes 1815556
  83.9 3.1 copy-start.62
  87.0 5.2 copy-start.12
  87.0 18.9 %slice-start = ((s8[4718592]{0:T(1024)(128)(4,1)}), s8[4194304]{0:T(1024)(128)(4,1)S(1)}, s32[]{:S(2)}) async-start(s8[4718592]{0:T(1024)(128)(4,1)} %bitcast.99), calls=%async_computation.11 | async-start | bytes 8388608
  92.2 13.7 %slice-start.1 = ((s8[4718592]{0:T(1024)(128)(4,1)}), s8[524288]{0:T(1024)(128)(4,1)S(1)}, s32[]{:S(2)}) async-start(s8[4718592]{0:T(1024)(128)(4,1)} %bitcast.99), calls=%async_computation.12 | async-start | bytes 1048576
  109.1 4.0 copy-start.43
  129.5 108.7 %reduce-scatter.15.cloned.1.call-start = ((), (), s32[]{:S(2)}) async-start(), calls=%async_computation.9 | async-start | bytes 884736
  146.4 4.2 copy-start.8
  163.6 7.1 copy-start.23
  164.3 6.4 copy-start.51
  164.3 6.4 copy-start.15
  164.3 6.4 copy-start.32
  164.3 6.4 copy-start.35
  164.3 6.4 copy-start.39
  164.3 6.4 copy-start.47
  175.4 122.2 %all-reduce.12.cloned.1.call-start = ((), (), s32[]{:S(2)}) async-start(), calls=%async_computation.10 | async-start | bytes 4915200 | tf_op jit(solution)/shard_map/psum | solution.py:100
  184.7 183.4 %reduce-scatter.13.cloned.1.call-start = ((), (), s32[]{:S(2)}) async-start(), calls=%async_computation.8 | async-start | bytes 2211840
  196.9 337.7 %reduce-scatter.9.cloned.1.call-start = ((), (), s32[]{:S(2)}) async-start(), calls=%async_computation.6 | async-start | bytes 10616832 | tf_op jit(solution)/shard_map/reduce_scatter | solution.py:166
  205.2 496.1 %reduce-scatter.11.cloned.1.call-start = ((), (), s32[]{:S(2)}) async-start(), calls=%async_computation.7 | async-start | bytes 10616832 | tf_op jit(solution)/shard_map/reduce_scatter | solution.py:167
  214.2 85.4 %copy-start.61 = (f32[768]{0:T(1024)S(1)}, f32[768]{0:T(1024)}, u32[]{:S(2)}) copy-start(f32[768]{0:T(1024)} %get-tuple-element.83) | copy-start | bytes 9220
  214.2 85.4 %copy-start.63 = (f32[4,768]{1,0:T(4,128)S(1)}, f32[4,768]{1,0:T(4,128)}, u32[]{:S(2)}) copy-start(f32[4,768]{1,0:T(4,128)} %get-tuple-element.80) | copy-start | bytes 36868
  (46 other events, 73.6 us)
Sparse Core Ops, SparseCore 0:
  19.0 40.6 all-reduce.7
  129.6 38.2 all-reduce.9
  175.5 62.6 reduce-scatter.14
  241.2 56.3 all-reduce.11
  301.3 66.7 reduce-scatter.12
  372.2 162.3 reduce-scatter.8
  538.8 162.5 reduce-scatter.10
where the time goes:
time: 716 us; the launch traced here: 708 us
  waiting for transfers between devices  465 us (65%)
  local copies, waits for them, and re-layouts  77.4 us (11%)
  matrix products  66.7 us (9%)
  blocking collectives  45.1 us (6%)
  other arithmetic  37.7 us (5%)
  between operations  16 us (2%)
    reduce_scatter x1, waiting for transfers between devices, body(): lax.psum_scatter(g_back, 'dp', scatter_dimension=2, tiled=True)  167 us
    reduce_scatter x1, waiting for transfers between devices, body(): lax.psum_scatter(g_in, 'dp', scatter_dimension=1, tiled=True)  165 us
    psum x1, waiting for transfers between devices, body(): moe, dots = lax.psum((moe_part, dots_part), 'tensor')  57.7 us
    unnamed x9, waiting for transfers between devices  47.9 us
    psum x1, blocking collectives, body(): lax.psum((g_norms, g_qv, g_bout, g_router, g_bin, g_bback), 'dp')  38.6 us
    psum x1, waiting for transfers between devices, body(): lax.psum(jnp.dot(context, w_out, preferred_element_type=jnp.float32), 'te...  24.3 us
    unnamed x151, local copies, waits for them, and re-layouts  18.1 us
  transfers between devices with their start and end apart: 7, of which 7 were waited for; matrix products, arithmetic and copies ran while one was open for 13% of the time, Pallas kernels for 0%

commit v1 on v0

--- a/solution.py
+++ b/solution.py
@@ -1,6 +1,8 @@
 import jax
 import jax.numpy as jnp
 from jax import lax
+from jax.experimental import pallas as pl
+from jax.experimental.pallas import tpu as pltpu
 from jax.sharding import PartitionSpec as P
 
 HD = 64
@@ -29,7 +31,7 @@
     return jax.nn.gelu(value, approximate=False)
 
 
-def body(
+def body_any(
     tokens,
     norm_params,
     w_qkv,
@@ -185,6 +187,431 @@
     )
 
 
+PAD = 208
+
+
+def send(value, axis, flip):
+    size = 8 if axis == "dp" else 4
+    return lax.ppermute(value, axis, [(i, i ^ flip) for i in range(size)])
+
+
+def pick(flag, one, two):
+    return jnp.where(flag == 0, one, two)
+
+
+def in_order(flag, mine, theirs, dim):
+    return pick(
+        flag, jnp.concatenate([mine, theirs], dim), jnp.concatenate([theirs, mine], dim)
+    )
+
+
+def mm(left, right):
+    return jnp.dot(left, right, preferred_element_type=jnp.float32)
+
+
+def mm_nt(left, right):
+    return lax.dot_general(left, right, (((1,), (1,)), ((), ())), preferred_element_type=jnp.float32)
+
+
+def pad_rows(value, images):
+    width = value.shape[-1]
+    return jnp.pad(value.reshape(images, SEQ, width), ((0, 0), (0, PAD - SEQ), (0, 0))).reshape(
+        images * PAD, width
+    )
+
+
+def cut_rows(value, images):
+    width = value.shape[-1]
+    return value.reshape(images, PAD, width)[:, :SEQ].reshape(images * SEQ, width)
+
+
+def block_of(value, index, size, dim):
+    return lax.dynamic_slice_in_dim(value, index * size, size, dim)
+
+
+ROOT_HALF = 0.7071067811865476
+ROOT_TWO_PI = 0.3989422804014327
+
+
+def expert_kernel(
+    at_ref, act_ref, dy_ref, weight_ref, w_in_ref, b_in_ref, w_back_ref, keep0_ref, send0_ref,
+    low_ref, dpre_ref, dots_ref, keep_ref, send_ref, bias_ref
+):
+    expert, core = at_ref[0], at_ref[1]
+    half = keep_ref.shape[1]
+    pre = jnp.dot(act_ref[...], w_in_ref[0], preferred_element_type=jnp.float32) + b_in_ref[0]
+    back = mm_nt(dy_ref[...], w_back_ref[0])
+    cdf = 0.5 + 0.5 * lax.erf(pre * ROOT_HALF)
+    low = (pre * cdf).astype(jnp.bfloat16)
+    low_ref[...] = low
+    lanes = jnp.zeros((low.shape[0], 128), jnp.float32)
+    for at in range(0, low.shape[1], 128):
+        lanes += low[:, at : at + 128].astype(jnp.float32) * back[:, at : at + 128]
+    dots_ref[0] = jnp.sum(lanes.T, 0, keepdims=True)
+    lane = lax.broadcasted_iota(jnp.int32, weight_ref.shape, 1)
+    weight = jnp.sum(jnp.where(lane == expert, weight_ref[...], 0.0), -1, keepdims=True)
+    slope = cdf + pre * (ROOT_TWO_PI * jnp.exp(-0.5 * pre * pre))
+    dpre = (back * weight * slope).astype(jnp.bfloat16)
+    dpre_ref[...] = dpre
+
+    @pl.when(pl.program_id(0) == 0)
+    def _():
+        bias_ref[...] = jnp.zeros_like(bias_ref)
+
+    bias_ref[...] += jnp.sum(dpre.astype(jnp.float32), 0, keepdims=True)
+    keep_at = pl.multiple_of(core * half, 128)
+    send_at = pl.multiple_of((1 - core) * half, 128)
+    keep_ref[...] = keep0_ref[...] + mm_nt(dpre, w_in_ref[0, pl.ds(keep_at, half), :])
+    send_ref[...] = send0_ref[...] + mm_nt(dpre, w_in_ref[0, pl.ds(send_at, half), :])
+
+
+def expert_pass(where, act, dy_low, weights, w_in, b_in, w_back, keep0, send0, tile):
+    rows, width = act.shape
+    hidden = w_in.shape[2]
+    half = width // 2
+    row = lambda n: pl.BlockSpec((tile, n), lambda i, at: (i, 0))
+    one = lambda a, b: pl.BlockSpec((1, a, b), lambda i, at: (at[0], 0, 0))
+    return pl.pallas_call(
+        expert_kernel,
+        out_shape=(
+            jax.ShapeDtypeStruct((rows, hidden), jnp.bfloat16),
+            jax.ShapeDtypeStruct((rows, hidden), jnp.bfloat16),
+            jax.ShapeDtypeStruct((rows // tile, 1, tile), jnp.float32),
+            jax.ShapeDtypeStruct((rows, half), jnp.float32),
+            jax.ShapeDtypeStruct((rows, half), jnp.float32),
+            jax.ShapeDtypeStruct((1, hidden), jnp.float32),
+        ),
+        grid_spec=pltpu.PrefetchScalarGridSpec(
+            num_scalar_prefetch=1,
+            grid=(rows // tile,),
+            in_specs=[
+                row(width),
+                row(width),
+                row(weights.shape[1]),
+                one(width, hidden),
+                one(1, hidden),
+                one(hidden, width),
+                row(half),
+                row(half),
+            ],
+            out_specs=(
+                row(hidden),
+                row(hidden),
+                pl.BlockSpec((1, 1, tile), lambda i, at: (i, 0, 0)),
+                row(half),
+                row(half),
+                pl.BlockSpec((1, hidden), lambda i, at: (0, 0)),
+            ),
+        ),
+        compiler_params=pltpu.CompilerParams(vmem_limit_bytes=48 * 2**20),
+        name="expert_pass",
+    )(where, act, dy_low, weights, w_in, b_in, w_back, keep0, send0)
+
+
+def after(value, *others):
+    return lax.optimization_barrier((value, *others))[0]
+
+
+def body_block(
+    tokens,
+    norm_params,
+    w_qkv,
+    b_qv,
+    w_out,
+    b_out,
+    w_router,
+    w_in,
+    b_in,
+    w_back,
+    b_back,
+    routes,
+    img_count,
+    cotangent,
+):
+    row_count, width = tokens.shape
+    images = row_count // SEQ
+    rows = images * PAD
+    cols = w_qkv.shape[2]
+    heads_loc = cols // HD
+    experts = w_in.shape[0]
+    mine = experts // 2
+    half = width // 2
+    part = width // 8
+    scale = HD ** (-0.5)
+    core = lax.axis_index("tensor") % 2
+    group = lax.axis_index("dp")
+    y_at = group % 2
+    z_low = (group // 2) % 2
+    z_high = group // 4
+
+    slot_of = jnp.arange(rows, dtype=jnp.int32)
+    inside = slot_of % PAD < SEQ
+    live = ((slot_of // PAD < img_count[0]) & inside).astype(jnp.float32)[:, None]
+    x_full = pad_rows(tokens, images).astype(jnp.float32)
+    dy = pad_rows(cotangent, images).astype(jnp.float32) * live
+    picks = jnp.sum(
+        (routes[:, :, None] == jnp.arange(experts, dtype=jnp.int32)[None, None, :]).astype(
+            jnp.float32
+        ),
+        1,
+    )
+    chosen = pad_rows(picks, images)
+
+    def to_partner(block):
+        got = send(block, "dp", 2)
+        return in_order(core, got, send(got, "tensor", 1), 1)
+
+    with_live = send(jnp.concatenate([chosen, live], 1).T, "dp", 2).T
+    chosen_there = with_live[:, :experts]
+    dy_there = to_partner(block_of(dy, core, half, 1)) * with_live[:, experts:]
+    w_back_two = block_of(w_back, z_low, mine, 0)
+
+    norm_one, normed_one, inv_one = normalize(x_full, norm_params[0], norm_params[1])
+    act_one = norm_one.astype(jnp.bfloat16)
+    project = jnp.einsum("rd,jdc->jrc", act_one, w_qkv, preferred_element_type=jnp.float32)
+    q_loc = (project[0] + b_qv[0]).astype(jnp.bfloat16).reshape(images, PAD, heads_loc, HD)
+    k_loc = project[1].astype(jnp.bfloat16).reshape(images, PAD, heads_loc, HD)
+    v_loc = (project[2] + b_qv[1]).astype(jnp.bfloat16).reshape(images, PAD, heads_loc, HD)
+    scores = scale * jnp.einsum("iqhd,ikhd->ihqk", q_loc, k_loc, preferred_element_type=jnp.float32)
+    key_ok = (jnp.arange(PAD) < SEQ)[None, None, None, :]
+    scores = jnp.where(key_ok, scores, -jnp.inf)
+    log_total = jax.nn.logsumexp(scores, axis=-1, keepdims=True)
+    probs = jnp.exp(scores - log_total)
+    probs_low = probs.astype(jnp.bfloat16)
+    context = jnp.einsum("ihqk,ikhd->iqhd", probs_low, v_loc, preferred_element_type=jnp.float32)
+    context = context.astype(jnp.bfloat16).reshape(rows, cols)
+
+    def sum_over_tensor(make):
+        got = send(make(1 - core), "tensor", 1)
+        total = make(core) + got
+        return total + send(total, "tensor", 2)
+
+    attn_half = sum_over_tensor(lambda at: mm(context, block_of(w_out, at, half, 1)))
+    hid_half = (
+        block_of(x_full, core, half, 1) + attn_half + lax.dynamic_slice_in_dim(b_out, core * half, half)
+    )
+    hidden = in_order(core, hid_half, send(hid_half, "tensor", 1), 1)
+    hid_there = to_partner(hid_half)
+
+    def route(value, pick_re):
+        normed, hat, inv = normalize(value, norm_params[2], norm_params[3])
+        low = normed.astype(jnp.bfloat16)
+        gates = jax.nn.softmax(mm(low, w_router), axis=-1)
+        return low, hat, inv, gates, gates * pick_re
+
+    act_two, normed_two, inv_two, gates, weights = route(hidden, chosen)
+    act_there, _, _, _, weights_there = route(hid_there, chosen_there)
+    act_all = jnp.concatenate([act_two, act_there], 0)
+    weights_all = jnp.concatenate([weights, weights_there], 0)
+    dy_all = jnp.concatenate([dy, dy_there], 0)
+    dy_low = dy_all.astype(jnp.bfloat16)
+    weights_two = block_of(weights_all, z_low, mine, 1)
+
+    act_t = act_all.T.reshape(4, 2, part, 2 * rows)
+    dy_t = dy_low.T.reshape(4, 2, part, 2 * rows)
+    def two_rows(left, at, count):
+        return lax.dynamic_index_in_dim(left, at, 1, keepdims=False).reshape(4 * part, count)
+
+    def first_send(left, right):
+        out = mm(two_rows(left, 1 - y_at, right.shape[0]), right).reshape(4, part, -1)
+        return out, send(out, "dp", 1)
+
+    def first_sum(left, right, got):
+        total = mm(two_rows(left, y_at, right.shape[0]), right).reshape(4, part, -1) + got
+        return block_of(total, z_high, 2, 0), block_of(total, 1 - z_high, 2, 0)
+
+    def split_low(pair):
+        return (
+            lax.dynamic_index_in_dim(pair, z_low, 0, keepdims=False),
+            lax.dynamic_index_in_dim(pair, 1 - z_low, 0, keepdims=False),
+        )
+
+    def du_of(e):
+        return (
+            dy_t.astype(jnp.float32) * weights_two[:, e][None, None, None, :]
+        ).astype(jnp.bfloat16)
+
+    hid_low, dpre, dots, g_bin_two = [], [], [], []
+    du_t = [du_of(e) for e in range(mine)]
+    sent, got_one = [], []
+    keep = away = jnp.zeros((2 * rows, half), jnp.float32)
+    act_in = act_all
+    for e in range(mine):
+        where = jnp.stack([z_low * mine + e, core]).astype(jnp.int32)
+        low, dp, dot, keep, away, bias = expert_pass(
+            where, act_in, dy_low, weights_all, w_in, b_in[:, None, :], w_back, keep, away, PAD
+        )
+        hid_low.append(low)
+        dpre.append(dp)
+        dots.append(dot.reshape(2 * rows))
+        g_bin_two.append(bias[0])
+        out, got = first_send(du_t[e], low)
+        sent.append(out)
+        got_one.append(got)
+        act_in = after(act_in, out)
+
+    def home(keep, away):
+        total = keep + send(away, "tensor", 1)
+        total = total[:rows] + send(total[rows:], "dp", 2)
+        return total + send(total, "tensor", 2)
+
+    total = keep + send(away, "tensor", 1)
+    total = after(total, sent[1])
+    got_total = send(total[rows:], "dp", 2)
+    mid = [first_sum(du_t[0], after(hid_low[0], total), got_one[0])]
+    got_mid = [send(mid[0][1], "dp", 4)]
+
+    def next_chunk(right):
+        out, got = first_send(act_t, right)
+        sent.append(out)
+        got_one.append(got)
+
+    def serve(left, right, at):
+        mid.append(first_sum(left, right, got_one[at]))
+        got_mid.append(send(mid[at][1], "dp", 4))
+
+    next_chunk(after(dpre[0], mid[0][1]))
+    total = after(total[:rows], mid[0][1], sent[2]) + got_total
+    got_total = send(total, "tensor", 2)
+    serve(du_t[1], after(hid_low[1], total), 1)
+    next_chunk(after(dpre[1], mid[1][1]))
+    hid_late = [after(low, total) for low in hid_low]
+    da2_half = after(total, mid[1][1], sent[3]) + got_total
+    da2_main = in_order(core, da2_half, send(da2_half, "tensor", 1), 1)
+    dots = jnp.stack(dots, 0)
+    dots = dots + send(dots, "tensor", 1)
+    dots = dots + send(dots, "tensor", 2)
+    dots = in_order(z_low, dots[:, :rows], send(dots[:, rows:], "dp", 2), 0)
+
+    dgates = (
+        dots.T + lax.dot_general(dy, b_back, (((1,), (1,)), ((), ())), precision=lax.Precision.HIGHEST)
+    ) * chosen
+    dlogits = gates * (dgates - jnp.sum(gates * dgates, -1, keepdims=True))
+    dlog_low = dlogits.astype(jnp.bfloat16)
+    da_two = da2_main + mm_nt(dlog_low, w_router)
+    dhid = dy + norm_back(da_two, normed_two, inv_two, norm_params[2])
+    dhid_low = dhid.astype(jnp.bfloat16)
+
+    def moe_columns(at):
+        total = jnp.zeros((2 * rows, half), jnp.float32)
+        for e in range(mine):
+            total = total + weights_two[:, e : e + 1] * mm(hid_late[e], block_of(w_back_two[e], at, half, 1))
+        return total
+
+    moe_half = home(moe_columns(core), moe_columns(1 - core))
+    moe = in_order(core, moe_half, send(moe_half, "tensor", 1), 1)
+    for e in range(experts):
+        moe = moe + weights[:, e : e + 1] * b_back[e]
+    out_act = cut_rows(((hidden + moe) * live).astype(jnp.bfloat16), images)
+
+    dcontext = mm_nt(dhid_low, w_out).astype(jnp.bfloat16).reshape(images, PAD, heads_loc, HD)
+    dprobs = jnp.einsum("iqhd,ikhd->ihqk", dcontext, v_loc, preferred_element_type=jnp.float32)
+    dv_loc = jnp.einsum(
+        "ihqk,iqhd->ikhd", probs_low, dcontext, preferred_element_type=jnp.float32
+    ).astype(jnp.bfloat16)
+    dscore = (probs * (dprobs - jnp.sum(probs * dprobs, -1, keepdims=True))).astype(jnp.bfloat16)
+    serve(act_t, after(dpre[0], dscore), 2)
+    dscore = after(dscore, mid[2][1])
+    dq_loc = (
+        scale * jnp.einsum("ihqk,ikhd->iqhd", dscore, k_loc, preferred_element_type=jnp.float32)
+    ).astype(jnp.bfloat16)
+    dk_loc = (
+        scale * jnp.einsum("ihqk,iqhd->ikhd", dscore, q_loc, preferred_element_type=jnp.float32)
+    ).astype(jnp.bfloat16)
+    dcat = jnp.concatenate([d.reshape(rows, cols) for d in (dq_loc, dk_loc, dv_loc)], 1)
+
+    def da1_columns(at):
+        w_at = block_of(w_qkv, at, half, 1)
+        return mm_nt(dcat, jnp.concatenate([w_at[0], w_at[1], w_at[2]], 1))
+
+    da1_send = da1_columns(1 - core)
+    da1_got = send(da1_send, "tensor", 1)
+    act_one_t = act_one.T.reshape(4, 2, part, rows)
+    q_sent, q_got = first_send(act_one_t, after(dcat, da1_send))
+    da1_keep = da1_columns(core)
+    norm_sums = []
+    for at_half in (0, 1):
+        piece = pick(core, da1_keep, da1_send) if at_half == 0 else pick(core, da1_send, da1_keep)
+        hat = normed_one[:, at_half * half : (at_half + 1) * half]
+        norm_sums.append(jnp.stack([jnp.sum(piece * hat, 0), jnp.sum(piece, 0)], 0))
+    norm_sums = jnp.concatenate(norm_sums, 1)
+    norm_sums = norm_sums + send(norm_sums, "tensor", 1)
+    da1_half = da1_keep + da1_got
+    da1_there = send(da1_half, "tensor", 2)
+    norm_sums = after(norm_sums, da1_half)
+    norm_sums = norm_sums + send(norm_sums, "tensor", 2)
+    serve(act_t, after(dpre[1], da1_half), 3)
+    da1_half = after(da1_half, mid[3][1]) + da1_there
+    da_one = in_order(core, da1_half, send(da1_half, "tensor", 1), 1)
+    in_grad = dhid + norm_back(da_one, normed_one, inv_one, norm_params[0])
+    in_grad = cut_rows(in_grad, images)
+    dhid_t = dhid_low.T.reshape(4, 2, part, rows)
+    o_sent, o_got = first_send(dhid_t, context)
+    q_mid = first_sum(act_one_t, after(dcat, mid[3][1]), q_got)
+    q_pair = q_mid[0] + send(q_mid[1], "dp", 4)
+    q_keep, q_away = split_low(q_pair)
+    g_qkv = (q_keep + send(q_away, "dp", 2)).reshape(part, 3, cols).swapaxes(0, 1)
+    o_mid = first_sum(dhid_t, context, o_got)
+    o_keep, o_away = split_low(o_mid[0] + send(o_mid[1], "dp", 4))
+    g_out = (o_keep + send(o_away, "dp", 2)).T
+
+    final = []
+    for pair, got in zip(mid, got_mid):
+        ours, theirs = split_low(pair[0] + got)
+        final.append((ours, send(theirs, "dp", 2)))
+
+    def assemble(pairs):
+        ours = jnp.stack([p[0] for p in pairs], 0)
+        theirs = jnp.stack([p[1] for p in pairs], 0)
+        return in_order(z_low, ours, theirs, 0)
+
+    g_back = jnp.swapaxes(assemble(final[:mine]), 1, 2)
+    g_in = assemble(final[mine:])
+
+    def all_groups(pack):
+        for flip in (1, 2, 4):
+            pack = pack + send(pack, "dp", flip)
+        return pack
+
+    g_router = mm(dlog_low.T, act_two)
+    g_bin_two = jnp.stack(g_bin_two, 0)
+    g_bin = in_order(z_low, g_bin_two, jnp.zeros_like(g_bin_two), 0)
+    g_bback = lax.dot_general(
+        weights, dy, (((0,), (0,)), ((), ())), precision=lax.Precision.HIGHEST
+    )
+    dsum = jnp.sum(dcat.astype(jnp.float32), 0)
+    pack = all_groups(
+        jnp.concatenate(
+            [
+                norm_sums,
+                jnp.sum(da_two * normed_two, 0)[None],
+                jnp.sum(da_two, 0)[None],
+                jnp.sum(dhid, 0)[None],
+                g_router,
+                g_bback,
+                g_bin,
+                jnp.pad(dsum, (0, width - 3 * cols))[None],
+            ],
+            0,
+        )
+    )
+    g_qv = jnp.stack([pack[-1, :cols], pack[-1, 2 * cols : 3 * cols]], 0)
+    return (
+        out_act,
+        in_grad,
+        pack[:4],
+        g_qkv,
+        g_qv,
+        g_out,
+        pack[4],
+        pack[5 : 5 + experts].T,
+        g_in,
+        pack[5 + 2 * experts : 5 + 3 * experts],
+        g_back,
+        pack[5 + experts : 5 + 2 * experts],
+    )
+
+
 def solution(mesh):
     placed = (
         P("dp", None),
@@ -202,6 +629,8 @@
         P("dp"),
         P("dp", None),
     )
+    sizes = dict(mesh.shape)
+    body = body_block if (sizes["dp"], sizes["tensor"]) == (8, 4) else body_any
     return jax.shard_map(
         body,
         mesh=mesh,

time: 716 us -> 338 us (0.47)
  waiting for transfers between devices: 465 us -> 136 us
  blocking collectives: 45.1 us -> 0 us
  starting transfers between devices: 0.68 us -> 39.5 us
  local copies, waits for them, and re-layouts: 77.4 us -> 53.7 us
  matrix products: 66.7 us -> 44.2 us
  Pallas kernels: 0 us -> 18.5 us
  between operations: 16 us -> 3.41 us
    reduce_scatter x2 -> x0, waiting for transfers between devices: 331 us -> none  [the longest x1 167 us: body(): lax.psum_scatter(g_back, 'dp', scatter_dimension=2, tiled=True)]
    ppermute x0 -> x45, waiting for transfers between devices: none -> 136 us  [send(): return lax.ppermute(value, axis, [(i, i ^ flip) for i in range(size)])]
    psum x3 -> x0, waiting for transfers between devices: 85.6 us -> none  [the longest x1 57.7 us: body(): moe, dots = lax.psum((moe_part, dots_part), 'tensor')]
    unnamed x9 -> x0, waiting for transfers between devices: 47.9 us -> none
    psum x2 -> x0, blocking collectives: 45.1 us -> none  [the longest x1 38.6 us: body(): lax.psum((g_norms, g_qv, g_bout, g_router, g_bin, g_bback), 'dp')]
    ppermute x0 -> x45, starting transfers between devices: none -> 39.5 us  [send(): return lax.ppermute(value, axis, [(i, i ^ flip) for i in range(size)])]
    dot_general x21 -> x33, matrix products: 63.5 us -> 43.6 us  [the longest x21 29.7 us: mm(): return jnp.dot(left, right, preferred_element_type=jnp.float32)]
    pallas_call x0 -> x2, Pallas kernels: none -> 18.5 us  [expert_pass(): pl.pallas_call(expert_kernel, out_shape=(jax.ShapeDtypeStruct((rows, hidd...]
  transfers between devices with their start and end apart: 7 -> 45, of which waited for: 7 -> 20; matrix products, arithmetic and copies ran while one was open for 13% -> 31% of each run, Pallas kernels for 0% -> 3%
where the time goes in v1:
time: 338 us; the launch traced here: 332 us
  waiting for transfers between devices  136 us (40%)
  local copies, waits for them, and re-layouts  53.7 us (16%)
  matrix products  44.2 us (13%)
  starting transfers between devices  39.5 us (12%)
  other arithmetic  35.8 us (11%)
  Pallas kernels  18.5 us (5%)
  between operations  3.41 us (1%)
    ppermute x45, waiting for transfers between devices, send(): return lax.ppermute(value, axis, [(i, i ^ flip) for i in range(size)])  136 us
    ppermute x45, starting transfers between devices, send(): return lax.ppermute(value, axis, [(i, i ^ flip) for i in range(size)])  39.5 us
    dot_general x21, matrix products, mm(): return jnp.dot(left, right, preferred_element_type=jnp.float32)  29.7 us
    pallas_call x2, Pallas kernels, expert_pass(): pl.pallas_call(expert_kernel, out_shape=(jax.ShapeDtypeStruct((rows, hidd...  18.5 us
    unnamed x204, local copies, waits for them, and re-layouts  12.5 us
  transfers between devices with their start and end apart: 45, of which 20 were waited for; matrix products, arithmetic and copies ran while one was open for 31% of the time, Pallas kernels for 3%

profile of v1, /device:TPU:0, one launch (start us, length us, event | category | flops | bytes accessed | tf_op | source)
XLA Modules:
  0.0 331.6 jit_solution(8453245932083364300)
XLA Ops:
  14.2 2.8 collective-permute-start.6
  21.3 11.0 %collective-permute-done.6 = f32[416,384]{1,0:T(8,128)} collective-permute-done((f32[416,384]{1,0:T(8,128)}, f32[416,384]{1,0:T(8,128)}, u32[]{:S(2)}, u32[]{:S(2)}) %collective-permute-start.6) | collective-permute-done | bytes 639008 | tf_op jit(solution)/shard_map/ppermute | solution.py:195
  33.9 2.2 dynamic-slice_bitcast_fusion.15
  43.6 2.2 copy.153
  48.4 2.2 convert_bitcast_fusion
  50.6 3.4 %copy.141 = f32[768,832]{1,0:T(8,128)} copy(f32[768,832]{0,1:T(8,128)} %get-tuple-element.155) | data formatting | bytes 5111808 | tf_op jit(solution)/shard_map/convert_element_type | solution.py:431
  62.1 3.4 %multiply_convert_fusion = (bf16[4,2,96,832]{3,2,1,0:T(8,128)(2,1)}, bf16[4,2,96,832]{3,2,1,0:T(8,128)(2,1)S(1)}) fusion(f32[4,2,96,832]{3,2,1,0:T(8,128)} %bitcast.230, f32[832]{0:T(1024)S(1)} %get-tuple-element.136, f32[832]{0:T(1024)S(1)} %get-tuple-element.137), kind=kLoop, calls=%fused_computation.1 | loop fusion | flops 2555904 | bytes 5118464 | tf_op jit(solution)/shard_map/convert_element_type | solution.py:432
  66.7 8.9 %expert_pass.2 = (bf16[832,768]{1,0:T(8,128)(2,1)S(1)}, bf16[832,768]{1,0:T(8,128)(2,1)S(1)}, f32[4,1,208]{2,1,0:T(1,128)S(1)}, f32[832,384]{1,0:T(8,128)S(1)}, ...) custom-call(s32[2]{0:T(128)S(1)} %get-tuple-element.193.at_ref, bf16[832,768]{1,0:T(8,128)(2,1)} %get-tuple-element.41.act_ref, ...), custom_call_target="tpu_custom_call" | custom-call | tf_op jit(solution)/shard_map/expert_pass/pallas_call | solution.py:274
  80.3 9.6 %expert_pass.3 = (bf16[832,768]{1,0:T(8,128)(2,1)S(1)}, bf16[832,768]{1,0:T(8,128)(2,1)S(1)}, f32[4,1,208]{2,1,0:T(1,128)S(1)}, f32[832,384]{1,0:T(8,128)S(1)}, ...) custom-call(s32[2]{0:T(128)S(1)} %get-tuple-element.194.at_ref, bf16[832,768]{1,0:T(8,128)(2,1)} %get-tuple-element.41.act_ref, ...), custom_call_target="tpu_custom_call" | custom-call | tf_op jit(solution)/shard_map/expert_pass/pallas_call | solution.py:274
  92.0 2.7 copy.143
  94.7 3.3 %fusion.24 = f32[4,96,768]{2,1,0:T(8,128)} fusion(bf16[832,768]{1,0:T(8,128)(2,1)} %copy-done.6, bf16[4,2,96,832]{3,2,1,0:T(8,128)(2,1)} %get-tuple-element.147, s32[]{:T(128)S(6)} %select_n.242), kind=kOutput, calls=%fused_computation.47 | convolution fusion | flops 490733568 | bytes 3145732 | tf_op jit(solution)/shard_map/dot_general | solution.py:209
  107.8 2.6 multiply_reduce_fusion.7
  115.5 2.3 convolution_add_fusion.3
  117.9 2.6 collective-permute-start.41
  123.8 17.3 %collective-permute-done.10 = f32[416,384]{1,0:T(8,128)S(1)} collective-permute-done((f32[416,384]{1,0:T(8,128)S(1)}, f32[416,384]{1,0:T(8,128)S(1)}, u32[]{:S(2)}, u32[]{:S(2)}) %collective-permute-start.10) | collective-permute-done | bytes 639008 | tf_op jit(solution)/shard_map/ppermute | solution.py:195
  141.3 2.1 convolution_add_fusion.2
  145.3 14.1 %collective-permute-done.41 = f32[2,96,768]{2,1,0:T(8,128)S(1)} collective-permute-done((f32[2,96,768]{2,1,0:T(8,128)S(1)}, f32[2,96,768]{2,1,0:T(8,128)S(1)}, u32[]{:S(2)}, u32[]{:S(2)}) %collective-permute-start.41) | collective-permute-done | bytes 589856 | tf_op jit(solution)/shard_map/ppermute | solution.py:195
  162.3 8.8 %collective-permute-done.42 = f32[2,96,768]{2,1,0:T(8,128)S(1)} collective-permute-done((f32[2,96,768]{2,1,0:T(8,128)S(1)}, f32[2,96,768]{2,1,0:T(8,128)S(1)}, u32[]{:S(2)}, u32[]{:S(2)}) %collective-permute-start.42) | collective-permute-done | bytes 589856 | tf_op jit(solution)/shard_map/ppermute | solution.py:195
  177.0 3.5 %collective-permute-done.44 = f32[96,768]{1,0:T(8,128)S(1)} collective-permute-done((f32[96,768]{1,0:T(8,128)S(1)}, f32[96,768]{1,0:T(8,128)S(1)}, u32[]{:S(2)}, u32[]{:S(2)}) %collective-permute-start.44) | collective-permute-done | bytes 294944 | tf_op jit(solution)/shard_map/ppermute | solution.py:195
  194.3 2.1 convolution_add_fusion.1
  197.3 3.6 %collective-permute-start.37 = (f32[2,96,768]{2,1,0:T(8,128)}, f32[2,96,768]{2,1,0:T(8,128)}, u32[]{:S(2)}, u32[]{:S(2)}) collective-permute-start(f32[2,96,768]{2,1,0:T(8,128)} %constant_dynamic-slice_fusion.7), channel_id=1, source_target_pairs={{0,16},{4,20},{8,24},{12,28},{16,0},{20,4},{24,8},{28,12},{1,17},{... | collective-permute-start | bytes 1769480 | tf_op jit(solution)/shard_map/ppermute | solution.py:195
  212.2 4.6 %collective-permute-done.34 = f32[4,96,192]{2,1,0:T(8,128)S(1)} collective-permute-done((f32[4,96,192]{2,1,0:T(8,128)S(1)}, f32[4,96,192]{2,1,0:T(8,128)S(1)}, u32[]{:S(2)}, u32[]{:S(2)}) %collective-permute-start.34) | collective-permute-done | bytes 294944 | tf_op jit(solution)/shard_map/ppermute | solution.py:195
  219.3 14.2 %collective-permute-done.35 = f32[2,96,192]{2,1,0:T(8,128)S(1)} collective-permute-done((f32[2,96,192]{2,1,0:T(8,128)S(1)}, f32[2,96,192]{2,1,0:T(8,128)S(1)}, u32[]{:S(2)}, u32[]{:S(2)}) %collective-permute-start.35) | collective-permute-done | bytes 147488 | tf_op jit(solution)/shard_map/ppermute | solution.py:195
  234.5 3.8 %collective-permute-done.36 = f32[96,192]{1,0:T(8,128)S(1)} collective-permute-done((f32[96,192]{1,0:T(8,128)S(1)}, f32[96,192]{1,0:T(8,128)S(1)}, u32[]{:S(2)}, u32[]{:S(2)}) %collective-permute-start.36) | collective-permute-done | bytes 73760 | tf_op jit(solution)/shard_map/ppermute | solution.py:195
  247.8 2.0 convolution_add_fusion
  251.9 8.0 %collective-permute-done.31 = f32[4,96,576]{2,1,0:T(8,128)} collective-permute-done((f32[4,96,576]{2,1,0:T(8,128)}, f32[4,96,576]{2,1,0:T(8,128)}, u32[]{:S(2)}, u32[]{:S(2)}) %collective-permute-start.31) | collective-permute-done | bytes 884768 | tf_op jit(solution)/shard_map/ppermute | solution.py:195
  262.9 8.1 %collective-permute-done.27 = f32[2,768]{1,0:T(2,128)S(1)} collective-permute-done((f32[2,768]{1,0:T(2,128)S(1)}, f32[2,768]{1,0:T(2,128)S(1)}, u32[]{:S(2)}, u32[]{:S(2)}) %collective-permute-start.27) | collective-permute-done | bytes 6176 | tf_op jit(solution)/shard_map/ppermute | solution.py:195
  271.5 18.2 %collective-permute-done.38 = f32[2,96,768]{2,1,0:T(8,128)S(1)} collective-permute-done((f32[2,96,768]{2,1,0:T(8,128)S(1)}, f32[2,96,768]{2,1,0:T(8,128)S(1)}, u32[]{:S(2)}, u32[]{:S(2)}) %collective-permute-start.38) | collective-permute-done | bytes 589856 | tf_op jit(solution)/shard_map/ppermute | solution.py:195
  290.7 9.4 %collective-permute-done.32 = f32[2,96,576]{2,1,0:T(8,128)S(1)} collective-permute-done((f32[2,96,576]{2,1,0:T(8,128)S(1)}, f32[2,96,576]{2,1,0:T(8,128)S(1)}, u32[]{:S(2)}, u32[]{:S(2)}) %collective-permute-start.32) | collective-permute-done | bytes 442400 | tf_op jit(solution)/shard_map/ppermute | solution.py:195
  301.4 6.3 %collective-permute-done.40 = f32[96,768]{1,0:T(8,128)S(1)} collective-permute-done((f32[96,768]{1,0:T(8,128)S(1)}, f32[96,768]{1,0:T(8,128)S(1)}, u32[]{:S(2)}, u32[]{:S(2)}) %collective-permute-start.40) | collective-permute-done | bytes 294944 | tf_op jit(solution)/shard_map/ppermute | solution.py:195
  310.8 2.8 fusion.159
  321.2 2.2 collective-permute-done.29
  (460 shorter events, 137.7 us)
Async XLA Ops:
  14.2 18.1 %collective-permute-start.6 = (f32[416,384]{1,0:T(8,128)}, f32[416,384]{1,0:T(8,128)}, u32[]{:S(2)}, u32[]{:S(2)}) collective-permute-start(f32[416,384]{1,0:T(8,128)} %constant_dynamic-slice_fusion.10), channel_id=1, source_target_pairs={{0,8},{4,12},{8,0},{12,4},{16,24},{20,28},{24,16},{28,20},{1,9},{5... | collective-permute-start | bytes 1916936 | tf_op jit(solution)/shard_map/ppermute | solution.py:195
  18.4 17.6 %collective-permute-start.1 = (f32[416,384]{1,0:T(8,128)S(1)}, f32[416,384]{1,0:T(8,128)S(1)}, u32[]{:S(2)}, u32[]{:S(2)}) collective-permute-start(f32[416,384]{1,0:T(8,128)S(1)} %convolution_add_fusion.5), channel_id=1, source_target_pairs={{0,2},{1,3},{2,0},{3,1},{4,6},{5,7},{6,4},{7,5},{8,10},{9,11},{10,... | collective-permute-start | bytes 1916936 | tf_op jit(solution)/shard_map/ppermute | solution.py:195
  20.8 25.0 %collective-permute-start.5 = (f32[5,416]{1,0:T(8,128)}, f32[5,416]{1,0:T(8,128)}, u32[]{:S(2)}, u32[]{:S(2)}) collective-permute-start(f32[5,416]{1,0:T(8,128)} %maximum_bitcast_fusion), channel_id=1, source_target_pairs={{0,8},{4,12},{8,0},{12,4},{16,24},{20,28},{24,16},{28,20},{1,9},{5... | collective-permute-start | bytes 24968 | tf_op jit(solution)/shard_map/ppermute | solution.py:195
  32.3 14.2 %collective-permute-start.7 = (f32[416,384]{1,0:T(8,128)}, f32[416,384]{1,0:T(8,128)}, u32[]{:S(2)}, u32[]{:S(2)}) collective-permute-start(f32[416,384]{1,0:T(8,128)} %collective-permute-done.6), channel_id=1, source_target_pairs={{0,1},{1,0},{2,3},{3,2},{4,5},{5,4},{6,7},{7,6},{8,9},{9,8},{10,11... | collective-permute-start | bytes 1916936 | tf_op jit(solution)/shard_map/ppermute | solution.py:195
  38.1 15.9 %collective-permute-start.2 = (f32[416,384]{1,0:T(8,128)S(1)}, f32[416,384]{1,0:T(8,128)S(1)}, u32[]{:S(2)}, u32[]{:S(2)}) collective-permute-start(f32[416,384]{1,0:T(8,128)S(1)} %add_add_fusion), channel_id=1, source_target_pairs={{0,1},{1,0},{2,3},{3,2},{4,5},{5,4},{6,7},{7,6},{8,9},{9,8},{10,11... | collective-permute-start | bytes 1916936 | tf_op jit(solution)/shard_map/ppermute | solution.py:195
  38.7 16.4 %collective-permute-start.3 = (f32[416,384]{1,0:T(8,128)S(1)}, f32[416,384]{1,0:T(8,128)S(1)}, u32[]{:S(2)}, u32[]{:S(2)}) collective-permute-start(f32[416,384]{1,0:T(8,128)S(1)} %add_add_fusion), channel_id=1, source_target_pairs={{0,8},{4,12},{8,0},{12,4},{16,24},{20,28},{24,16},{28,20},{1,9},{5... | collective-permute-start | bytes 1916936 | tf_op jit(solution)/shard_map/ppermute | solution.py:195
  78.6 36.9 %collective-permute-start.9 = (f32[4,96,768]{2,1,0:T(8,128)}, f32[4,96,768]{2,1,0:T(8,128)}, u32[]{:S(2)}, u32[]{:S(2)}) collective-permute-start(f32[4,96,768]{2,1,0:T(8,128)} %fusion.26), channel_id=1, source_target_pairs={{0,4},{4,0},{8,12},{12,8},{16,20},{20,16},{24,28},{28,24},{1,5},{5... | collective-permute-start | bytes 3538952 | tf_op jit(solution)/shard_map/ppermute | solution.py:195
  92.0 20.3 %collective-permute-start.8 = (f32[832,384]{1,0:T(8,128)}, f32[832,384]{1,0:T(8,128)}, u32[]{:S(2)}, u32[]{:S(2)}) collective-permute-start(f32[832,384]{1,0:T(8,128)} %get-tuple-element.45), channel_id=1, source_target_pairs={{0,1},{1,0},{2,3},{3,2},{4,5},{5,4},{6,7},{7,6},{8,9},{9,8},{10,11... | collective-permute-start | bytes 3833864 | tf_op jit(solution)/shard_map/ppermute | solution.py:195
  98.0 43.2 %collective-permute-start.15 = (f32[4,96,768]{2,1,0:T(8,128)}, f32[4,96,768]{2,1,0:T(8,128)}, u32[]{:S(2)}, u32[]{:S(2)}) collective-permute-start(f32[4,96,768]{2,1,0:T(8,128)} %fusion.24), channel_id=1, source_target_pairs={{0,4},{4,0},{8,12},{12,8},{16,20},{20,16},{24,28},{28,24},{1,5},{5... | collective-permute-start | bytes 3538952 | tf_op jit(solution)/shard_map/ppermute | solution.py:195
  113.9 27.3 %collective-permute-start.10 = (f32[416,384]{1,0:T(8,128)S(1)}, f32[416,384]{1,0:T(8,128)S(1)}, u32[]{:S(2)}, u32[]{:S(2)}) collective-permute-start(f32[416,384]{1,0:T(8,128)S(1)} %get-tuple-element.151), channel_id=1, source_target_pairs={{0,8},{4,12},{8,0},{12,4},{16,24},{20,28},{24,16},{28,20},{1,9},{5... | collective-permute-start | bytes 1916936 | tf_op jit(solution)/shard_map/ppermute | solution.py:195
  117.9 41.5 %collective-permute-start.41 = (f32[2,96,768]{2,1,0:T(8,128)S(1)}, f32[2,96,768]{2,1,0:T(8,128)S(1)}, u32[]{:S(2)}, u32[]{:S(2)}) collective-permute-start(f32[2,96,768]{2,1,0:T(8,128)S(1)} %constant_dynamic-slice_fusion.9), channel_id=1, source_target_pairs={{0,16},{4,20},{8,24},{12,28},{16,0},{20,4},{24,8},{28,12},{1,17},{... | collective-permute-start | bytes 1769480 | tf_op jit(solution)/shard_map/ppermute | solution.py:195
  122.3 71.2 %collective-permute-start.21 = (f32[4,96,768]{2,1,0:T(8,128)}, f32[4,96,768]{2,1,0:T(8,128)}, u32[]{:S(2)}, u32[]{:S(2)}) collective-permute-start(f32[4,96,768]{2,1,0:T(8,128)} %fusion.21), channel_id=1, source_target_pairs={{0,4},{4,0},{8,12},{12,8},{16,20},{20,16},{24,28},{28,24},{1,5},{5... | collective-permute-start | bytes 3538952 | tf_op jit(solution)/shard_map/ppermute | solution.py:195
  143.4 27.7 %collective-permute-start.42 = (f32[2,96,768]{2,1,0:T(8,128)S(1)}, f32[2,96,768]{2,1,0:T(8,128)S(1)}, u32[]{:S(2)}, u32[]{:S(2)}) collective-permute-start(f32[2,96,768]{2,1,0:T(8,128)S(1)} %constant_dynamic-slice_fusion.8), channel_id=1, source_target_pairs={{0,16},{4,20},{8,24},{12,28},{16,0},{20,4},{24,8},{28,12},{1,17},{... | collective-permute-start | bytes 1769480 | tf_op jit(solution)/shard_map/ppermute | solution.py:195
  145.2 36.4 %collective-permute-start.11 = (f32[832,384]{1,0:T(8,128)S(1)}, f32[832,384]{1,0:T(8,128)S(1)}, u32[]{:S(2)}, u32[]{:S(2)}) collective-permute-start(f32[832,384]{1,0:T(8,128)S(1)} %fusion.3), channel_id=1, source_target_pairs={{0,1},{1,0},{2,3},{3,2},{4,5},{5,4},{6,7},{7,6},{8,9},{9,8},{10,11... | collective-permute-start | bytes 3833864 | tf_op jit(solution)/shard_map/ppermute | solution.py:195
  159.5 15.9 %collective-permute-start.43 = (f32[96,768]{1,0:T(8,128)S(1)}, f32[96,768]{1,0:T(8,128)S(1)}, u32[]{:S(2)}, u32[]{:S(2)}) collective-permute-start(f32[96,768]{1,0:T(8,128)S(1)} %get-tuple-element.169), channel_id=1, source_target_pairs={{0,8},{4,12},{8,0},{12,4},{16,24},{20,28},{24,16},{28,20},{1,9},{5... | collective-permute-start | bytes 884744 | tf_op jit(solution)/shard_map/ppermute | solution.py:195
  160.8 12.5 %collective-permute-start.16 = (f32[416,384]{1,0:T(8,128)S(1)}, f32[416,384]{1,0:T(8,128)S(1)}, u32[]{:S(2)}, u32[]{:S(2)}) collective-permute-start(f32[416,384]{1,0:T(8,128)S(1)} %add.389), channel_id=1, source_target_pairs={{0,2},{1,3},{2,0},{3,1},{4,6},{5,7},{6,4},{7,5},{8,10},{9,11},{10,... | collective-permute-start | bytes 1916936 | tf_op jit(solution)/shard_map/ppermute | solution.py:195
  175.5 72.4 %collective-permute-start.23 = (f32[4,96,768]{2,1,0:T(8,128)}, f32[4,96,768]{2,1,0:T(8,128)}, u32[]{:S(2)}, u32[]{:S(2)}) collective-permute-start(f32[4,96,768]{2,1,0:T(8,128)} %fusion.18), channel_id=1, source_target_pairs={{0,4},{4,0},{8,12},{12,8},{16,20},{20,16},{24,28},{28,24},{1,5},{5... | collective-permute-start | bytes 3538952 | tf_op jit(solution)/shard_map/ppermute | solution.py:195
  183.5 58.5 %collective-permute-start.12 = (f32[416,384]{1,0:T(8,128)}, f32[416,384]{1,0:T(8,128)}, u32[]{:S(2)}, u32[]{:S(2)}) collective-permute-start(f32[416,384]{1,0:T(8,128)} %slice.203), channel_id=1, source_target_pairs={{0,8},{4,12},{8,0},{12,4},{16,24},{20,28},{24,16},{28,20},{1,9},{5... | collective-permute-start | bytes 1916936 | tf_op jit(solution)/shard_map/ppermute | solution.py:195
  197.3 43.2 %collective-permute-start.37 = (f32[2,96,768]{2,1,0:T(8,128)}, f32[2,96,768]{2,1,0:T(8,128)}, u32[]{:S(2)}, u32[]{:S(2)}) collective-permute-start(f32[2,96,768]{2,1,0:T(8,128)} %constant_dynamic-slice_fusion.7), channel_id=1, source_target_pairs={{0,16},{4,20},{8,24},{12,28},{16,0},{20,4},{24,8},{28,12},{1,17},{... | collective-permute-start | bytes 1769480 | tf_op jit(solution)/shard_map/ppermute | solution.py:195
  212.2 32.5 %collective-permute-start.22 = (f32[416,384]{1,0:T(8,128)}, f32[416,384]{1,0:T(8,128)}, u32[]{:S(2)}, u32[]{:S(2)}) collective-permute-start(f32[416,384]{1,0:T(8,128)} %fusion.77), channel_id=1, source_target_pairs={{0,1},{1,0},{2,3},{3,2},{4,5},{5,4},{6,7},{7,6},{8,9},{9,8},{10,11... | collective-permute-start | bytes 1916936 | tf_op jit(solution)/shard_map/ppermute | solution.py:195
  217.1 16.4 %collective-permute-start.35 = (f32[2,96,192]{2,1,0:T(8,128)S(1)}, f32[2,96,192]{2,1,0:T(8,128)S(1)}, u32[]{:S(2)}, u32[]{:S(2)}) collective-permute-start(f32[2,96,192]{2,1,0:T(8,128)S(1)} %constant_dynamic-slice_fusion.4), channel_id=1, source_target_pairs={{0,16},{4,20},{8,24},{12,28},{16,0},{20,4},{24,8},{28,12},{1,17},{... | collective-permute-start | bytes 442376 | tf_op jit(solution)/shard_map/ppermute | solution.py:195
  238.3 21.6 %collective-permute-start.31 = (f32[4,96,576]{2,1,0:T(8,128)}, f32[4,96,576]{2,1,0:T(8,128)}, u32[]{:S(2)}, u32[]{:S(2)}) collective-permute-start(f32[4,96,576]{2,1,0:T(8,128)} %fusion.68), channel_id=1, source_target_pairs={{0,4},{4,0},{8,12},{12,8},{16,20},{20,16},{24,28},{28,24},{1,5},{5... | collective-permute-start | bytes 2654216 | tf_op jit(solution)/shard_map/ppermute | solution.py:195
  243.5 46.4 %collective-permute-start.13 = (f32[416,384]{1,0:T(8,128)S(1)}, f32[416,384]{1,0:T(8,128)S(1)}, u32[]{:S(2)}, u32[]{:S(2)}) collective-permute-start(f32[416,384]{1,0:T(8,128)S(1)} %slice_add_fusion.1), channel_id=1, source_target_pairs={{0,2},{1,3},{2,0},{3,1},{4,6},{5,7},{6,4},{7,5},{8,10},{9,11},{10,... | collective-permute-start | bytes 1916936 | tf_op jit(solution)/shard_map/ppermute | solution.py:195
  246.8 24.5 %collective-permute-start.24 = (f32[416,384]{1,0:T(8,128)S(1)}, f32[416,384]{1,0:T(8,128)S(1)}, u32[]{:S(2)}, u32[]{:S(2)}) collective-permute-start(f32[416,384]{1,0:T(8,128)S(1)} %get-tuple-element.62), channel_id=1, source_target_pairs={{0,2},{1,3},{2,0},{3,1},{4,6},{5,7},{6,4},{7,5},{8,10},{9,11},{10,... | collective-permute-start | bytes 1916936 | tf_op jit(solution)/shard_map/ppermute | solution.py:195
  250.0 39.7 %collective-permute-start.38 = (f32[2,96,768]{2,1,0:T(8,128)S(1)}, f32[2,96,768]{2,1,0:T(8,128)S(1)}, u32[]{:S(2)}, u32[]{:S(2)}) collective-permute-start(f32[2,96,768]{2,1,0:T(8,128)S(1)} %constant_dynamic-slice_fusion.6), channel_id=1, source_target_pairs={{0,16},{4,20},{8,24},{12,28},{16,0},{20,4},{24,8},{28,12},{1,17},{... | collective-permute-start | bytes 1769480 | tf_op jit(solution)/shard_map/ppermute | solution.py:195
  250.9 20.1 %collective-permute-start.27 = (f32[2,768]{1,0:T(2,128)S(1)}, f32[2,768]{1,0:T(2,128)S(1)}, u32[]{:S(2)}, u32[]{:S(2)}) collective-permute-start(f32[2,768]{1,0:T(2,128)S(1)} %fusion.191), channel_id=1, source_target_pairs={{0,2},{1,3},{2,0},{3,1},{4,6},{5,7},{6,4},{7,5},{8,10},{9,11},{10,... | collective-permute-start | bytes 18440 | tf_op jit(solution)/shard_map/ppermute | solution.py:195
  261.7 38.4 %collective-permute-start.32 = (f32[2,96,576]{2,1,0:T(8,128)S(1)}, f32[2,96,576]{2,1,0:T(8,128)S(1)}, u32[]{:S(2)}, u32[]{:S(2)}) collective-permute-start(f32[2,96,576]{2,1,0:T(8,128)S(1)} %constant_dynamic-slice_fusion.5), channel_id=1, source_target_pairs={{0,16},{4,20},{8,24},{12,28},{16,0},{20,4},{24,8},{28,12},{1,17},{... | collective-permute-start | bytes 1327112 | tf_op jit(solution)/shard_map/ppermute | solution.py:195
  271.0 30.4 %collective-permute-start.39 = (f32[96,768]{1,0:T(8,128)S(1)}, f32[96,768]{1,0:T(8,128)S(1)}, u32[]{:S(2)}, u32[]{:S(2)}) collective-permute-start(f32[96,768]{1,0:T(8,128)S(1)} %get-tuple-element.173), channel_id=1, source_target_pairs={{0,8},{4,12},{8,0},{12,4},{16,24},{20,28},{24,16},{28,20},{1,9},{5... | collective-permute-start | bytes 884744 | tf_op jit(solution)/shard_map/ppermute | solution.py:195
  271.4 37.5 %collective-permute-start.25 = (f32[416,384]{1,0:T(8,128)S(1)}, f32[416,384]{1,0:T(8,128)S(1)}, u32[]{:S(2)}, u32[]{:S(2)}) collective-permute-start(f32[416,384]{1,0:T(8,128)S(1)} %add.411), channel_id=1, source_target_pairs={{0,1},{1,0},{2,3},{3,2},{4,5},{5,4},{6,7},{7,6},{8,9},{9,8},{10,11... | collective-permute-start | bytes 1916936 | tf_op jit(solution)/shard_map/ppermute | solution.py:195
  289.8 18.0 %collective-permute-start.40 = (f32[96,768]{1,0:T(8,128)S(1)}, f32[96,768]{1,0:T(8,128)S(1)}, u32[]{:S(2)}, u32[]{:S(2)}) collective-permute-start(f32[96,768]{1,0:T(8,128)S(1)} %get-tuple-element.175), channel_id=1, source_target_pairs={{0,8},{4,12},{8,0},{12,4},{16,24},{20,28},{24,16},{28,20},{1,9},{5... | collective-permute-start | bytes 884744 | tf_op jit(solution)/shard_map/ppermute | solution.py:195
  290.7 28.4 %collective-permute-start.14 = (f32[416,384]{1,0:T(8,128)}, f32[416,384]{1,0:T(8,128)}, u32[]{:S(2)}, u32[]{:S(2)}) collective-permute-start(f32[416,384]{1,0:T(8,128)} %add.394), channel_id=1, source_target_pairs={{0,1},{1,0},{2,3},{3,2},{4,5},{5,4},{6,7},{7,6},{8,9},{9,8},{10,11... | collective-permute-start | bytes 1916936 | tf_op jit(solution)/shard_map/ppermute | solution.py:195
  301.0 14.3 %collective-permute-start.33 = (f32[96,576]{1,0:T(8,128)}, f32[96,576]{1,0:T(8,128)}, u32[]{:S(2)}, u32[]{:S(2)}) collective-permute-start(f32[96,576]{1,0:T(8,128)} %dynamic-slice_bitcast_fusion.12), channel_id=1, source_target_pairs={{0,8},{4,12},{8,0},{12,4},{16,24},{20,28},{24,16},{28,20},{1,9},{5... | collective-permute-start | bytes 663560 | tf_op jit(solution)/shard_map/ppermute | solution.py:195
  (113 other events, 727.5 us)
